TPU v7x, 32 devices: a whole 2x2x4 slice. The times are simulated.
32 devices in a mesh: dp: 4 (over x, core), seq: 8 (over z, y).
Axes of the slice: x: 2, y: 2, z: 4, core: 2. Of those that a mesh axis runs over, the one named last changes fastest.
Arguments:
- patches: bfloat16 [4, 4096, 6144], P('dp', 'seq'), may hold values from -6 to 6
- embedding: bfloat16 [6144, 768], P('seq'), may hold values from -0.078125 to 0.078125
- first_gain: bfloat16 [768], P('seq'), may hold values from 0.5 to 1.5
- first_shift: bfloat16 [768], P('seq'), may hold values from -4 to 4
- joint_weight: bfloat16 [768, 2304], P('seq'), may hold values from -0.3125 to 0.3125
- output_weight: bfloat16 [768, 768], P('seq'), may hold values from -0.875 to 0.875
- second_gain: bfloat16 [768], P('seq'), may hold values from 0.5 to 1.5
- second_shift: bfloat16 [768], P('seq'), may hold values from -4 to 4
- up_weight: bfloat16 [768, 3072], P('seq'), may hold values from -0.21875 to 0.21875
- up_bias: bfloat16 [3072], P('seq'), may hold values from -6 to 6
- down_weight: bfloat16 [3072, 768], P('seq'), may hold values from -0.109375 to 0.109375
- down_bias: bfloat16 [768], P('seq'), may hold values from -6 to 6
- block_number: int32 [4, 4096], P('dp'), may hold values from 0 to 31, never falling along the last dimension, each value on 1 to 256 neighbouring positions
- cotangent: bfloat16 [4, 4096, 768], P('dp', 'seq'), may hold values from -6 to 6
Outputs:
- block_output: bfloat16 [4, 4096, 768], P('dp', 'seq')
- patches_gradient: bfloat16 [4, 4096, 6144], P('dp', 'seq')
- embedding_gradient: float32 [6144, 768], P('seq')
- first_gain_gradient: float32 [768], P('seq')
- first_shift_gradient: float32 [768], P('seq')
- joint_weight_gradient: float32 [768, 2304], P('seq')
- output_weight_gradient: float32 [768, 768], P('seq')
- second_gain_gradient: float32 [768], P('seq')
- second_shift_gradient: float32 [768], P('seq')
- up_weight_gradient: float32 [768, 3072], P('seq')
- up_bias_gradient: float32 [3072], P('seq')
- down_weight_gradient: float32 [3072, 768], P('seq')
- down_bias_gradient: float32 [768], P('seq')
Inputs may be any that keep to these rules, and one draw needn't show every extreme that they name: `block_number`: in each sequence the block numbers never fall along the rows; each block has 1 to 256 rows, and some block has exactly 256.
All inputs are finite; a program needn't handle non-finite values.
Results may differ from a plain program's by a relative error of at most 0.038.
Values may be sent and summed in bfloat16 or wider, within the bound.
No kernel may reach another device: no remote copies, remote signals or barrier semaphores. Data moves between devices by JAX's collectives and lax.ppermute only.
A program may use at most 256 MiB of HBM per device.

v0:
```python
import math
import jax
import jax.numpy as jnp
from jax import lax
from jax.sharding import PartitionSpec as P

HEADS = 12
HEAD_DIM = 64
EPS = 1e-05
NEG = -1e30


def layer_norm(values, gain, shift):
    center = values - jnp.mean(values, axis=-1, keepdims=True)
    spread = jnp.mean(center * center, axis=-1, keepdims=True)
    return center * lax.rsqrt(spread + EPS) * gain + shift


def gelu_tanh(values):
    return jax.nn.gelu(values, approximate=True)


def masked_scores(query, keys, query_ids, key_ids, scale):
    scores = jnp.einsum("sqhd,skhd->shqk", query, keys, preferred_element_type=jnp.float32) * scale
    visible = key_ids[:, None, None, :] <= query_ids[:, None, :, None]
    return jnp.where(visible, scores, NEG)


def per_device(
    patches,
    embedding,
    first_gain,
    first_shift,
    joint_weight,
    output_weight,
    second_gain,
    second_shift,
    up_weight,
    up_bias,
    down_weight,
    down_bias,
    block_number,
    cotangent,
):
    seqs_here, rows_here, width_in = patches.shape
    model = HEADS * HEAD_DIM
    count_rows = seqs_here * rows_here
    length = block_number.shape[1]
    scale = HEAD_DIM ** (-0.5)
    gathered_params = (
        lax.all_gather(embedding, "seq", axis=0, tiled=True),
        lax.all_gather(first_gain, "seq", axis=0, tiled=True),
        lax.all_gather(first_shift, "seq", axis=0, tiled=True),
        lax.all_gather(joint_weight, "seq", axis=0, tiled=True),
        lax.all_gather(output_weight, "seq", axis=0, tiled=True),
        lax.all_gather(second_gain, "seq", axis=0, tiled=True),
        lax.all_gather(second_shift, "seq", axis=0, tiled=True),
        lax.all_gather(up_weight, "seq", axis=0, tiled=True),
        lax.all_gather(up_bias, "seq", axis=0, tiled=True),
        lax.all_gather(down_weight, "seq", axis=0, tiled=True),
        lax.all_gather(down_bias, "seq", axis=0, tiled=True),
    )
    (
        embed_full,
        gain_one,
        shift_one,
        joint_full,
        output_full,
        gain_two,
        shift_two,
        up_full,
        upbias_full,
        down_full,
        downbias_full,
    ) = gathered_params
    flat_in = patches.reshape(count_rows, width_in)
    hidden = jnp.dot(flat_in, embed_full, preferred_element_type=jnp.float32)
    normed1 = layer_norm(
        hidden, gain_one.astype(jnp.float32), shift_one.astype(jnp.float32)
    ).astype(jnp.bfloat16)
    joint = jnp.dot(normed1, joint_full, preferred_element_type=jnp.float32).astype(jnp.bfloat16)
    query = joint[:, :model].reshape(seqs_here, rows_here, HEADS, HEAD_DIM)
    local_pairs = joint[:, model:].reshape(seqs_here, rows_here, 2 * model)
    sequence_pairs = lax.all_gather(local_pairs, "seq", axis=1, tiled=True)
    keys_all = sequence_pairs[:, :, :model].reshape(seqs_here, length, HEADS, HEAD_DIM)
    values_all = sequence_pairs[:, :, model:].reshape(seqs_here, length, HEADS, HEAD_DIM)
    offset = lax.axis_index("seq") * rows_here
    query_ids = lax.dynamic_slice_in_dim(block_number, offset, rows_here, 1)
    last_ids = query_ids[:, -1]
    reach = jnp.max(jnp.sum((block_number <= last_ids[:, None]).astype(jnp.int32), axis=1))
    key_width = math.gcd(length, 512)
    starts = jnp.arange(length // key_width, dtype=jnp.int32) * key_width

    def key_slice(start, width):
        keys = lax.dynamic_slice_in_dim(keys_all, start, width, 1)
        values = lax.dynamic_slice_in_dim(values_all, start, width, 1)
        key_ids = lax.dynamic_slice_in_dim(block_number, start, width, 1)
        return (keys, values, key_ids)

    def total_step(carry, start):

        def total_visit(state):
            top, total = state
            keys, values, key_ids = key_slice(start, key_width)
            scores = masked_scores(query, keys, query_ids, key_ids, scale)
            new_top = jnp.maximum(top, jnp.max(scores, axis=-1))
            total = total * jnp.exp(top - new_top) + jnp.sum(
                jnp.exp(scores - new_top[..., None]), axis=-1
            )
            return (new_top, total)

        return (lax.cond(start < reach, total_visit, lambda state: state, carry), None)

    start_top = jnp.full((seqs_here, HEADS, rows_here), NEG, jnp.float32)
    start_total = jnp.zeros((seqs_here, HEADS, rows_here), jnp.float32)
    (top, total), _ = lax.scan(total_step, (start_top, start_total), starts)
    log_total = top + jnp.log(total)

    def output_step(accum, start):

        def output_visit(acc):
            keys, values, key_ids = key_slice(start, key_width)
            probs = jnp.exp(
                masked_scores(query, keys, query_ids, key_ids, scale) - log_total[..., None]
            ).astype(jnp.bfloat16)
            return acc + jnp.einsum(
                "shqk,skhd->sqhd", probs, values, preferred_element_type=jnp.float32
            )

        return (lax.cond(start < reach, output_visit, lambda acc: acc, accum), None)

    zero_query = jnp.zeros((seqs_here, rows_here, HEADS, HEAD_DIM), jnp.float32)
    attended, _ = lax.scan(output_step, zero_query, starts)
    attended_low = attended.reshape(count_rows, model).astype(jnp.bfloat16)
    resid = hidden + jnp.dot(attended_low, output_full, preferred_element_type=jnp.float32)
    gain_second = gain_two.astype(jnp.float32)
    shift_second = shift_two.astype(jnp.float32)
    normed2 = layer_norm(resid, gain_second, shift_second).astype(jnp.bfloat16)
    upper = jnp.dot(normed2, up_full, preferred_element_type=jnp.float32) + upbias_full.astype(
        jnp.float32
    )
    gate = gelu_tanh(upper).astype(jnp.bfloat16)
    lowered = jnp.dot(gate, down_full, preferred_element_type=jnp.float32) + downbias_full.astype(
        jnp.float32
    )
    block_output = (resid + lowered).astype(jnp.bfloat16).reshape(seqs_here, rows_here, model)
    again_params = (
        lax.all_gather(embedding, "seq", axis=0, tiled=True),
        lax.all_gather(first_gain, "seq", axis=0, tiled=True),
        lax.all_gather(first_shift, "seq", axis=0, tiled=True),
        lax.all_gather(joint_weight, "seq", axis=0, tiled=True),
        lax.all_gather(output_weight, "seq", axis=0, tiled=True),
        lax.all_gather(second_gain, "seq", axis=0, tiled=True),
        lax.all_gather(second_shift, "seq", axis=0, tiled=True),
        lax.all_gather(up_weight, "seq", axis=0, tiled=True),
        lax.all_gather(up_bias, "seq", axis=0, tiled=True),
        lax.all_gather(down_weight, "seq", axis=0, tiled=True),
        lax.all_gather(down_bias, "seq", axis=0, tiled=True),
    )
    (
        embed_back,
        gain_one_back,
        shift_one_back,
        joint_back,
        output_back,
        gain_two_back,
        shift_two_back,
        up_back,
        upbias_back,
        down_back,
        downbias_back,
    ) = again_params
    tangent = cotangent.reshape(count_rows, model)
    down_bias_grad = jnp.sum(tangent.astype(jnp.float32), axis=0)
    down_weight_grad = jnp.dot(gate.T, tangent, preferred_element_type=jnp.float32)
    gate_grad = jnp.dot(tangent, down_back.T, preferred_element_type=jnp.float32)
    _, gelu_pull = jax.vjp(gelu_tanh, upper)
    upper_grad = gelu_pull(gate_grad)[0].astype(jnp.bfloat16)
    up_bias_grad = jnp.sum(upper_grad.astype(jnp.float32), axis=0)
    up_weight_grad = jnp.dot(normed2.T, upper_grad, preferred_element_type=jnp.float32)
    normed2_grad = jnp.dot(upper_grad, up_back.T, preferred_element_type=jnp.float32)
    _, second_pull = jax.vjp(
        layer_norm, resid, gain_two_back.astype(jnp.float32), shift_two_back.astype(jnp.float32)
    )
    resid_part, second_gain_grad, second_shift_grad = second_pull(normed2_grad)
    resid_grad = tangent.astype(jnp.float32) + resid_part
    mixed_grad = resid_grad.astype(jnp.bfloat16)
    output_weight_grad = jnp.dot(attended_low.T, mixed_grad, preferred_element_type=jnp.float32)
    attended_grad = jnp.dot(mixed_grad, output_back.T, preferred_element_type=jnp.float32).astype(
        jnp.bfloat16
    )
    attended_grad = attended_grad.reshape(seqs_here, rows_here, HEADS, HEAD_DIM)
    delta = jnp.transpose(jnp.sum(attended_grad.astype(jnp.float32) * attended, axis=-1), (0, 2, 1))

    def score_pieces(start, width):
        keys, values, key_ids = key_slice(start, width)
        probs = jnp.exp(
            masked_scores(query, keys, query_ids, key_ids, scale) - log_total[..., None]
        )
        prob_grad = jnp.einsum(
            "sqhd,skhd->shqk", attended_grad, values, preferred_element_type=jnp.float32
        )
        score_grad = (probs * (prob_grad - delta[..., None])).astype(jnp.bfloat16)
        return (keys, probs, score_grad)

    def query_from(keys, score_grad):
        return (
            jnp.einsum("shqk,skhd->sqhd", score_grad, keys, preferred_element_type=jnp.float32)
            * scale
        )

    def pair_from(probs, score_grad, width):
        rounded = probs.astype(jnp.bfloat16)
        value_grad = jnp.einsum(
            "shqk,sqhd->skhd", rounded, attended_grad, preferred_element_type=jnp.float32
        )
        key_grad = (
            jnp.einsum("shqk,sqhd->skhd", score_grad, query, preferred_element_type=jnp.float32)
            * scale
        )
        paired = jnp.concatenate(
            [
                key_grad.reshape(seqs_here, width, model),
                value_grad.reshape(seqs_here, width, model),
            ],
            axis=-1,
        )
        return jnp.transpose(paired, (1, 0, 2))

    def both_grads(start, width):
        keys, probs, score_grad = score_pieces(start, width)
        return (query_from(keys, score_grad), pair_from(probs, score_grad, width))

    def whole_step(accum, start):
        empty_pair = jnp.zeros((key_width, seqs_here, 2 * model), jnp.float32)
        query_part, paired = lax.cond(
            start < reach, lambda: both_grads(start, key_width), lambda: (zero_query, empty_pair)
        )
        return (accum + query_part, paired)

    query_total, stacked = lax.scan(whole_step, zero_query, starts)
    every_pair = stacked.reshape(length, seqs_here, 2 * model)
    own_pairs = lax.psum_scatter(
        every_pair.astype(jnp.bfloat16), "seq", scatter_dimension=0, tiled=True
    ).astype(jnp.float32)
    pair_local = jnp.transpose(own_pairs, (1, 0, 2)).reshape(count_rows, 2 * model)
    joint_grad = jnp.concatenate(
        [query_total.reshape(count_rows, model), pair_local], axis=-1
    ).astype(jnp.bfloat16)
    joint_weight_grad = jnp.dot(normed1.T, joint_grad, preferred_element_type=jnp.float32)
    normed1_grad = jnp.dot(joint_grad, joint_back.T, preferred_element_type=jnp.float32)
    _, first_pull = jax.vjp(
        layer_norm, hidden, gain_one_back.astype(jnp.float32), shift_one_back.astype(jnp.float32)
    )
    hidden_part, first_gain_grad, first_shift_grad = first_pull(normed1_grad)
    hidden_grad = (resid_grad + hidden_part).astype(jnp.bfloat16)
    embedding_grad = jnp.dot(flat_in.T, hidden_grad, preferred_element_type=jnp.float32)
    patches_grad = jnp.dot(hidden_grad, embed_back.T, preferred_element_type=jnp.float32).astype(
        jnp.bfloat16
    )
    patches_grad = patches_grad.reshape(seqs_here, rows_here, width_in)
    group_terms = (
        lax.psum_scatter(
            embedding_grad.astype(jnp.bfloat16), "seq", scatter_dimension=0, tiled=True
        ).astype(jnp.float32),
        lax.psum_scatter(
            first_gain_grad.astype(jnp.bfloat16), "seq", scatter_dimension=0, tiled=True
        ).astype(jnp.float32),
        lax.psum_scatter(
            first_shift_grad.astype(jnp.bfloat16), "seq", scatter_dimension=0, tiled=True
        ).astype(jnp.float32),
        lax.psum_scatter(
            joint_weight_grad.astype(jnp.bfloat16), "seq", scatter_dimension=0, tiled=True
        ).astype(jnp.float32),
        lax.psum_scatter(
            output_weight_grad.astype(jnp.bfloat16), "seq", scatter_dimension=0, tiled=True
        ).astype(jnp.float32),
        lax.psum_scatter(
            second_gain_grad.astype(jnp.bfloat16), "seq", scatter_dimension=0, tiled=True
        ).astype(jnp.float32),
        lax.psum_scatter(
            second_shift_grad.astype(jnp.bfloat16), "seq", scatter_dimension=0, tiled=True
        ).astype(jnp.float32),
        lax.psum_scatter(
            up_weight_grad.astype(jnp.bfloat16), "seq", scatter_dimension=0, tiled=True
        ).astype(jnp.float32),
        lax.psum_scatter(
            up_bias_grad.astype(jnp.bfloat16), "seq", scatter_dimension=0, tiled=True
        ).astype(jnp.float32),
        lax.psum_scatter(
            down_weight_grad.astype(jnp.bfloat16), "seq", scatter_dimension=0, tiled=True
        ).astype(jnp.float32),
        lax.psum_scatter(
            down_bias_grad.astype(jnp.bfloat16), "seq", scatter_dimension=0, tiled=True
        ).astype(jnp.float32),
    )
    totals = (
        lax.psum(group_terms[0].astype(jnp.bfloat16), "dp").astype(jnp.float32),
        lax.psum(group_terms[1].astype(jnp.bfloat16), "dp").astype(jnp.float32),
        lax.psum(group_terms[2].astype(jnp.bfloat16), "dp").astype(jnp.float32),
        lax.psum(group_terms[3].astype(jnp.bfloat16), "dp").astype(jnp.float32),
        lax.psum(group_terms[4].astype(jnp.bfloat16), "dp").astype(jnp.float32),
        lax.psum(group_terms[5].astype(jnp.bfloat16), "dp").astype(jnp.float32),
        lax.psum(group_terms[6].astype(jnp.bfloat16), "dp").astype(jnp.float32),
        lax.psum(group_terms[7].astype(jnp.bfloat16), "dp").astype(jnp.float32),
        lax.psum(group_terms[8].astype(jnp.bfloat16), "dp").astype(jnp.float32),
        lax.psum(group_terms[9].astype(jnp.bfloat16), "dp").astype(jnp.float32),
        lax.psum(group_terms[10].astype(jnp.bfloat16), "dp").astype(jnp.float32),
    )
    return (
        block_output,
        patches_grad,
        totals[0],
        totals[1],
        totals[2],
        totals[3],
        totals[4],
        totals[5],
        totals[6],
        totals[7],
        totals[8],
        totals[9],
        totals[10],
    )


def solution(mesh):
    placed = (
        P("dp", "seq", None),
        P("seq", None),
        P("seq"),
        P("seq"),
        P("seq", None),
        P("seq", None),
        P("seq"),
        P("seq"),
        P("seq", None),
        P("seq"),
        P("seq", None),
        P("seq"),
        P("dp", None),
        P("dp", "seq", None),
    )
    return jax.shard_map(
        per_device,
        mesh=mesh,
        in_specs=placed,
        out_specs=(
            P("dp", "seq", None),
            P("dp", "seq", None),
            P("seq", None),
            P("seq"),
            P("seq"),
            P("seq", None),
            P("seq", None),
            P("seq"),
            P("seq"),
            P("seq", None),
            P("seq"),
            P("seq", None),
            P("seq"),
        ),
        check_vma=False,
    )
```

profile of v0, /device:TPU:0, one launch (start us, length us, event | category | flops | bytes accessed | tf_op | source)
XLA Modules:
  0.0 1777.7 jit_solution(17283474801182536518)
XLA Ops:
  14.1 24.6 %all-reduce.12 = (bf16[768]{0:T(1024)(128)(2,1)S(1)}, bf16[768]{0:T(1024)(128)(2,1)S(1)}, bf16[768]{0:T(1024)(128)(2,1)S(1)}, bf16[768]{0:T(1024)(128)(2,1)S(1)}) all-reduce(bf16[768]{0:T(1024)(128)(2,1)S(1)} %dynamic-update-slice.1, bf16[768]{0:T(1024)(128)(2,1)S(1)} %dynamic-update-slice, ...), channel_id=1, replica_groups=mesh['dp'=4,'seq'=8] {'seq'}, use_global_device_ids=true, to_apply=%add.1 | all-reduce | flops 3072 | bytes 12288
  38.7 112.0 %all-gather.9.cloned.1.call-done = bf16[6144,768]{1,0:T(8,128)(2,1)} async-done(((bf16[768,768]{1,0:T(8,128)(2,1)}), bf16[6144,768]{1,0:T(8,128)(2,1)}) %all-gather.9.cloned.1.call-update) | async-done | bytes 9437200 | tf_op jit(solution)/shard_map/all_gather | solution.py:51
  150.7 9.7 fusion.81
  160.8 54.9 %all-gather.11.cloned.1.call-done = bf16[768,2304]{1,0:T(8,128)(2,1)} async-done(((bf16[96,2304]{1,0:T(8,128)(2,1)}), bf16[768,2304]{1,0:T(8,128)(2,1)}) %all-gather.11.cloned.1.call-update) | async-done | bytes 3538960 | tf_op jit(solution)/shard_map/all_gather | solution.py:54
  215.7 4.1 convolution_convert_fusion.5
  224.4 27.1 %all-gather.1 = bf16[8,1,384]{2,1,0:T(2,128)(2,1)S(1)} all-gather(bf16[1,1,384]{2,1,0:T(2,128)(2,1)S(1)} %reshape.385), channel_id=1, replica_groups=mesh['dp'=4,'seq'=8] {'seq'}, dimensions={0}, use_global_device_ids=true | all-gather | bytes 6912 | tf_op jit(solution)/shard_map/all_gather | solution.py:59
  254.6 143.0 %all-gather.19.cloned.1.call-done = bf16[4096,1536]{1,0:T(8,128)(2,1)} async-done(((bf16[512,1536]{1,0:T(8,128)(2,1)}), bf16[4096,1536]{1,0:T(8,128)(2,1)}) %all-gather.19.cloned.1.call-update) | async-done | bytes 12582928 | tf_op jit(solution)/shard_map/all_gather | solution.py:84
  397.6 10.2 fusion.79
  407.8 8.7 copy.68
  416.5 8.6 copy.67
  425.1 35.6 %while.38 = (s32[]{:T(128)}, f32[1,12,512]{2,1,0:T(8,128)S(1)}, f32[1,12,512]{2,1,0:T(8,128)S(1)}, s32[8]{0:T(128)S(1)}, s32[]{:T(128)}, /*index=5*/s32[1,4096]{...) while((s32[]{:T(128)}, f32[1,12,512]{2,1,0:T(8,128)S(1)}, ...), condition=%wide.region_8.0_spmd, body=%wide.region_3.8_spmd.sunk | while | flops 424947712 | bytes 27853072 | solution.py:116
  427.0 10.1 conditional.7
  429.3 5.2 fusion
  434.5 2.6 exponential_reduce_fusion
  439.0 10.1 conditional.7
  441.3 5.2 fusion
  446.6 2.6 exponential_reduce_fusion
  460.9 33.7 %while.39 = (s32[]{:T(128)}, f32[1,512,12,64]{1,3,2,0:T(8,128)S(1)}, s32[8]{0:T(128)S(1)}, s32[]{:T(128)}, bf16[1,4096,12,64]{1,3,2,0:T(8,128)(2,1)}, /*index=5*...) while((s32[]{:T(128)}, ...), condition=%wide.region_12.13_spmd, body=%wide.region_9.0_spmd.sunk | while | flops 818544640 | bytes 6063357 | solution.py:133
  462.8 8.9 conditional.8
  465.1 6.7 bitcast_add_fusion.1
  473.7 9.0 conditional.8
  475.9 6.8 bitcast_add_fusion.1
  499.5 19.6 %all-gather.15.cloned.1.call-done = bf16[768,3072]{1,0:T(8,128)(2,1)} async-done(((bf16[96,3072]{1,0:T(8,128)(2,1)}), bf16[768,3072]{1,0:T(8,128)(2,1)}) %all-gather.15.cloned.1.call-update) | async-done | bytes 4718608 | tf_op jit(solution)/shard_map/all_gather | solution.py:58
  519.1 8.1 fusion.76
  527.2 71.7 %all-gather.17.cloned.1.call-done = bf16[3072,768]{1,0:T(8,128)(2,1)} async-done(((bf16[384,768]{1,0:T(8,128)(2,1)}), bf16[3072,768]{1,0:T(8,128)(2,1)}) %all-gather.17.cloned.1.call-update) | async-done | bytes 4718608 | tf_op jit(solution)/shard_map/all_gather | solution.py:60
  598.9 9.8 fusion.83
  608.6 3.5 multiply_reduce_fusion
  618.6 125.4 %while.40 = (s32[]{:T(128)}, f32[1,512,12,64]{1,3,2,0:T(8,128)}, bf16[8,512,1,1536]{3,1,0,2:T(8,128)(2,1)}, s32[8]{0:T(128)S(1)}, s32[]{:T(128)}, /*index=5*/bf1...) while((s32[]{:T(128)}, f32[1,512,12,64]{1,3,2,0:T(8,128)}, ...), condition=%wide.region_21.22_spmd.clone, body=%wide.region_18.0_spmd.clone.sunk | while | flops 2050097152 | bytes 80298304 | solution.py:241
  620.7 35.1 %conditional.9 = (f32[1,512,12,64]{1,3,2,0:T(8,128)S(1)}, bf16[1,512,1,1536]{1,3,2,0:T(8,128)(2,1)S(1)}) conditional(s32[]{:T(128)} %convert_element_type.293, () %tuple.107, (s32[]{:T(128)}, bf16[1,4096,12,64]{1,3,2,0:T(8,128)(2,1)}, s32[1,4096]{1,0:T(1,128)S(1)}, s32[1,512]{1,0:T(1,128)S(1)}, bf16[1,512,12,64]{1,3,2,0:T(8,128)(2,1)}, ...), branch_computations={%region_19.19_spmd, %region_20.20_spmd} | conditional | flops 2049310720 | bytes 69288000 | solution.py:236
  622.9 9.6 fusion.39
  632.5 9.7 fusion.28
  642.2 7.8 fusion.32
  650.0 2.5 multiply_bitcast_fusion
  652.5 3.1 convolution_multiply_fusion
  661.1 35.1 %conditional.9 = (f32[1,512,12,64]{1,3,2,0:T(8,128)S(1)}, bf16[1,512,1,1536]{1,3,2,0:T(8,128)(2,1)S(1)}) conditional(s32[]{:T(128)} %convert_element_type.293, () %tuple.107, (s32[]{:T(128)}, bf16[1,4096,12,64]{1,3,2,0:T(8,128)(2,1)}, s32[1,4096]{1,0:T(1,128)S(1)}, s32[1,512]{1,0:T(1,128)S(1)}, bf16[1,512,12,64]{1,3,2,0:T(8,128)(2,1)}, ...), branch_computations={%region_19.19_spmd, %region_20.20_spmd} | conditional | flops 2049310720 | bytes 69288000 | solution.py:236
  663.4 9.5 fusion.39
  673.0 9.7 fusion.28
  682.7 7.8 fusion.32
  690.5 2.5 multiply_bitcast_fusion
  693.0 3.1 convolution_multiply_fusion
  696.2 2.9 select_add_fusion.2
  703.3 2.9 select_add_fusion.2
  710.4 2.9 select_add_fusion.2
  717.6 2.9 select_add_fusion.2
  724.6 2.9 select_add_fusion.2
  731.8 2.9 select_add_fusion.2
  738.9 2.9 select_add_fusion.2
  747.3 6.5 convolution_convert_fusion.3
  754.9 8.6 convolution_convert_fusion.2
  767.3 413.9 %reduce-scatter.7.cloned.1.call-done = bf16[512,1,1536]{2,0,1:T(8,128)(2,1)} async-done(((bf16[4096,1,1536]{2,0,1:T(8,128)(2,1)}), bf16[512,1,1536]{2,0,1:T(8,128)(2,1)}) %reduce-scatter.7.cloned.1.call-update) | async-done | bytes 1572880 | tf_op jit(solution)/shard_map/reduce_scatter | solution.py:243
  1181.2 5.5 convolution_convert_fusion.4
  1186.8 4.8 multiply_reduce_fusion.1
  1193.6 10.6 fusion.51
  1206.1 35.3 %all-reduce.11 = (bf16[768]{0:T(1024)(128)(2,1)S(1)}, bf16[768]{0:T(1024)(128)(2,1)S(1)}, bf16[768]{0:T(1024)(128)(2,1)S(1)}, bf16[768]{0:T(1024)(128)(2,1)S(1)}...) all-reduce(bf16[768]{0:T(1024)(128)(2,1)S(1)} %dynamic-update-slice, ...), channel_id=1, replica_groups=mesh['dp'=4,'seq'=8] {'seq'}, use_global_device_ids=true, to_apply=%add.4 | all-reduce | flops 7680 | bytes 30720
  1241.4 7.7 reduce-scatter.13.cloned.1.call-done
  1249.0 98.9 %reduce-scatter.15.cloned.1.call-done = bf16[96,3072]{1,0:T(8,128)(2,1)} async-done(((bf16[768,3072]{1,0:T(8,128)(2,1)}), bf16[96,3072]{1,0:T(8,128)(2,1)}) %reduce-scatter.15.cloned.1.call-update) | async-done | bytes 589840 | tf_op jit(solution)/shard_map/reduce_scatter | solution.py:284
  1348.0 98.9 %reduce-scatter.17.cloned.1.call-done = bf16[384,768]{1,0:T(8,128)(2,1)} async-done(((bf16[3072,768]{1,0:T(8,128)(2,1)}), bf16[384,768]{1,0:T(8,128)(2,1)}) %reduce-scatter.17.cloned.1.call-update) | async-done | bytes 589840 | tf_op jit(solution)/shard_map/reduce_scatter | solution.py:290
  1446.8 82.7 %reduce-scatter.11.cloned.1.call-done = bf16[96,2304]{1,0:T(8,128)(2,1)} async-done(((bf16[768,2304]{1,0:T(8,128)(2,1)}), bf16[96,2304]{1,0:T(8,128)(2,1)}) %reduce-scatter.11.cloned.1.call-update) | async-done | bytes 442384 | tf_op jit(solution)/shard_map/reduce_scatter | solution.py:272
  1529.6 165.2 %reduce-scatter.9.cloned.1.call-done = bf16[768,768]{0,1:T(8,128)(2,1)} async-done(((bf16[6144,768]{0,1:T(8,128)(2,1)}), bf16[768,768]{0,1:T(8,128)(2,1)}) %reduce-scatter.9.cloned.1.call-update) | async-done | bytes 1179664 | tf_op jit(solution)/shard_map/reduce_scatter | solution.py:263
  1694.8 9.0 fusion.64
  1704.3 7.3 all-reduce.13
  1714.7 10.8 fusion.52
  1725.4 36.6 %all-reduce.17.cloned.1.call-done = (bf16[768,768]{0,1:T(8,128)(2,1)}, bf16[96,2304]{1,0:T(8,128)(2,1)}, bf16[96,768]{1,0:T(8,128)(2,1)}, bf16[96,3072]{1,0:T(8,128)(2,1)}, bf16[384,768]{1,0:T(8,128)(2,1)}) async-done(((bf16[768,768]{0,1:T(8,128)(2,1)}, bf16[96,2304]{1,0:T(8,128)(2,1)}, bf16[96,768]{1,0:T(8,128)(2,1)}, bf16[96,3072]{1,0:T(8,128)(2,1)}, bf16[384,768]{1,0:T(8,128)(2,1)}), ...) | async-done | bytes 2949136 | tf_op jit(solution)/shard_map/psum | solution.py:298
  1765.8 2.7 copy.73
  (277 shorter events, 82.7 us)
Async XLA Ops:
  7.2 143.5 %all-gather.9.cloned.1.call-start = ((), (), s32[]{:S(2)}) async-start(), calls=%async_computation.6 | async-start | bytes 10616832 | tf_op jit(solution)/shard_map/all_gather | solution.py:51
  7.9 207.8 %all-gather.11.cloned.1.call-start = ((), (), s32[]{:S(2)}) async-start(), calls=%async_computation.7 | async-start | bytes 3981312 | tf_op jit(solution)/shard_map/all_gather | solution.py:54
  8.7 388.9 %all-gather.19.cloned.1.call-start = ((), (), s32[]{:S(2)}) async-start(), calls=%async_computation.17 | async-start | bytes 14155776 | tf_op jit(solution)/shard_map/all_gather | solution.py:84
  38.7 177.0 %copy-start.34 = (f32[768]{0:T(1024)}, f32[768]{0:T(1024)S(1)}, u32[]{:S(2)}) copy-start(f32[768]{0:T(1024)S(1)} %convert_element_type.201) | copy-start | bytes 9220
  38.7 177.0 %copy-start.27 = (f32[768]{0:T(1024)}, f32[768]{0:T(1024)S(1)}, u32[]{:S(2)}) copy-start(f32[768]{0:T(1024)S(1)} %convert_element_type.200) | copy-start | bytes 9220
  160.4 335.2 %copy-start.1 = (f32[512,768]{1,0:T(8,128)}, f32[512,768]{1,0:T(8,128)S(1)}, u32[]{:S(2)}) copy-start(f32[512,768]{1,0:T(8,128)S(1)} %get-tuple-element.512) | copy-start | bytes 4718596
  160.5 59.4 %copy-start.21 = (f32[512]{0:T(512)}, f32[512]{0:T(512)S(1)}, u32[]{:S(2)}) copy-start(f32[512]{0:T(512)S(1)} %broadcast_multiply_fusion.1) | copy-start | bytes 6148
  160.8 59.1 %copy-start.23 = (f32[512]{0:T(512)}, f32[512]{0:T(512)S(1)}, u32[]{:S(2)}) copy-start(f32[512]{0:T(512)S(1)} %multiply_reduce_fusion.6) | copy-start | bytes 6148
  160.8 59.1 %copy-start.31 = (f32[512]{0:T(512)}, f32[512]{0:T(512)S(1)}, u32[]{:S(2)}) copy-start(f32[512]{0:T(512)S(1)} %fusion.72) | copy-start | bytes 6148
  219.8 1.4 copy-start.14
  221.3 3.1 copy-start.40
  221.3 30.3 %copy-start.20 = (s32[1,4096]{1,0:T(1,128)S(1)}, s32[1,4096]{1,0:T(1,128)}, u32[]{:S(2)}) copy-start(s32[1,4096]{1,0:T(1,128)} %param.38) | copy-start | bytes 49156
  222.5 30.9 %slice-start = ((bf16[512,2304]{1,0:T(8,128)(2,1)}), bf16[512,768]{1,0:T(8,128)(2,1)S(1)}, s32[]{:S(2)}) async-start(bf16[512,2304]{1,0:T(8,128)(2,1)} %copy-done.14), calls=%async_computation.19 | async-start | bytes 1572864 | tf_op jit(solution)/shard_map/slice | solution.py:82
  222.5 273.1 %all-gather.13.cloned.1.call-start = ((), (), s32[]{:S(2)}) async-start(), calls=%async_computation.8 | async-start | bytes 1327104 | tf_op jit(solution)/shard_map/all_gather | solution.py:55
  223.1 296.0 %all-gather.15.cloned.1.call-start = ((), (), s32[]{:S(2)}) async-start(), calls=%async_computation.9 | async-start | bytes 5308416 | tf_op jit(solution)/shard_map/all_gather | solution.py:58
  223.7 375.2 %all-gather.17.cloned.1.call-start = ((), (), s32[]{:S(2)}) async-start(), calls=%async_computation.10 | async-start | bytes 5308416 | tf_op jit(solution)/shard_map/all_gather | solution.py:60
  224.3 956.9 %reduce-scatter.7.cloned.1.call-start = ((), (), s32[]{:S(2)}) async-start(), calls=%async_computation.11 | async-start | bytes 14155776 | tf_op jit(solution)/shard_map/reduce_scatter | solution.py:243
  224.4 294.7 %copy-start.36 = (f32[768]{0:T(1024)}, f32[768]{0:T(1024)S(1)}, u32[]{:S(2)}) copy-start(f32[768]{0:T(1024)S(1)} %convert_element_type.207) | copy-start | bytes 9220
  251.5 347.4 %copy-start.29 = (f32[8,1,384]{2,1,0:T(1,128)}, f32[8,1,384]{2,1,0:T(1,128)S(1)}, u32[]{:S(2)}) copy-start(f32[8,1,384]{2,1,0:T(1,128)S(1)} %convert_element_type.243) | copy-start | bytes 36868
  498.1 1.1 copy-start.3
  499.5 99.4 %copy-start.9 = (bf16[1,512,768]{2,1,0:T(8,128)(2,1)S(1)}, bf16[1,512,768]{2,1,0:T(8,128)(2,1)}, u32[]{:S(2)}) copy-start(bf16[1,512,768]{2,1,0:T(8,128)(2,1)} %param.39) | copy-start | bytes 2359300
  598.9 9.8 copy-start.4
  598.9 9.8 copy-start.41
  608.6 3.5 copy-start.43
  612.2 3.0 copy-start.15
  612.8 1.2 copy-start.7
  612.9 3.1 copy-start.25
  614.3 0.9 copy-start.16
  744.0 1.1 copy-start.13
  744.0 1.4 copy-start.17
  744.1 3.2 copy-start.5
  744.1 3.2 copy-start.37
  744.1 504.9 %reduce-scatter.13.cloned.1.call-start = ((), (), s32[]{:S(2)}) async-start(), calls=%async_computation.14 | async-start | bytes 1327104 | tf_op jit(solution)/shard_map/reduce_scatter | solution.py:275
  747.2 600.7 %reduce-scatter.15.cloned.1.call-start = ((), (), s32[]{:S(2)}) async-start(), calls=%async_computation.15 | async-start | bytes 5308416 | tf_op jit(solution)/shard_map/reduce_scatter | solution.py:284
  753.8 1.1 copy-start.10
  753.8 1.1 copy-start.30
  753.8 693.1 %reduce-scatter.17.cloned.1.call-start = ((), (), s32[]{:S(2)}) async-start(), calls=%async_computation.16 | async-start | bytes 5308416 | tf_op jit(solution)/shard_map/reduce_scatter | solution.py:290
  763.5 1.4 copy-start
  763.5 417.7 %copy-start.2 = (f32[512,768]{1,0:T(8,128)S(1)}, f32[512,768]{1,0:T(8,128)}, u32[]{:S(2)}) copy-start(f32[512,768]{1,0:T(8,128)} %copy-done.1) | copy-start | bytes 4718596
  763.5 417.7 %copy-start.22 = (f32[512]{0:T(512)S(1)}, f32[512]{0:T(512)}, u32[]{:S(2)}) copy-start(f32[512]{0:T(512)} %copy-done.21) | copy-start | bytes 6148
  763.5 417.7 %copy-start.28 = (f32[768]{0:T(1024)S(1)}, f32[768]{0:T(1024)}, u32[]{:S(2)}) copy-start(f32[768]{0:T(1024)} %copy-done.27) | copy-start | bytes 9220
  763.5 417.7 %copy-start.32 = (f32[512]{0:T(512)S(1)}, f32[512]{0:T(512)}, u32[]{:S(2)}) copy-start(f32[512]{0:T(512)} %copy-done.31) | copy-start | bytes 6148
  763.5 417.7 %copy-start.35 = (f32[768]{0:T(1024)S(1)}, f32[768]{0:T(1024)}, u32[]{:S(2)}) copy-start(f32[768]{0:T(1024)} %copy-done.34) | copy-start | bytes 9220
  763.5 766.0 %reduce-scatter.11.cloned.1.call-start = ((), (), s32[]{:S(2)}) async-start(), calls=%async_computation.13 | async-start | bytes 3981312 | tf_op jit(solution)/shard_map/reduce_scatter | solution.py:272
  1186.7 4.9 copy-start.24
  1186.7 508.0 %reduce-scatter.9.cloned.1.call-start = ((), (), s32[]{:S(2)}) async-start(), calls=%async_computation.12 | async-start | bytes 10616832 | tf_op jit(solution)/shard_map/reduce_scatter | solution.py:263
  1191.6 1.4 copy-start.8
  1191.6 1.6 copy-start.11
  1191.6 1.6 copy-start.26
  1204.1 1.6 copy-start.12
  1204.1 1.7 copy-start.42
  1204.1 2.0 copy-start.33
  1204.2 2.0 copy-start.38
  1204.2 2.0 copy-start.39
  1204.2 490.6 %copy-start.6 = (f32[512,768]{1,0:T(8,128)S(1)}, f32[512,768]{1,0:T(8,128)}, u32[]{:S(2)}) copy-start(f32[512,768]{1,0:T(8,128)} %copy-done.3) | copy-start | bytes 4718596
  1204.2 557.9 %all-reduce.17.cloned.1.call-start = ((), (), s32[]{:S(2)}) async-start(), calls=%async_computation.18 | async-start | bytes 5898240 | tf_op jit(solution)/shard_map/psum | solution.py:298
  1762.1 6.5 copy-start.19
  1763.8 5.9 copy-start.18
Sparse Core Ops, SparseCore 0:
  10.2 140.4 all-gather.8
  152.9 62.7 all-gather.10
  222.7 174.8 all-gather.18
  399.6 39.2 all-gather.12
  441.0 78.0 all-gather.14
  521.1 77.6 all-gather.16
  744.2 436.9 reduce-scatter.6
  1185.1 63.8 reduce-scatter.12
  1253.3 94.6 reduce-scatter.14
  1351.5 95.3 reduce-scatter.16
  1450.5 79.0 reduce-scatter.10
  1533.0 161.7 reduce-scatter.8
  1697.5 64.5 all-reduce.16
where the time goes:
time: 1790 us; the launch traced here: 1780 us
  waiting for transfers between devices  1310 us (73%)
  matrix products  185 us (10%)
  blocking collectives  94.2 us (5%)
  local copies, waits for them, and re-layouts  82.7 us (5%)
  other arithmetic  45.2 us (3%)
  loops' own time  44.7 us (2%)
    reduce_scatter x1, waiting for transfers between devices, per_device(): lax.psum_scatter(every_pair.astype(jnp.bfloat16), 'seq', scatter_dimensio...  414 us
    reduce_scatter x1, waiting for transfers between devices, per_device(): lax.psum_scatter(embedding_grad.astype(jnp.bfloat16), 'seq', scatter_dime...  165 us
    all_gather x1, waiting for transfers between devices, per_device(): sequence_pairs = lax.all_gather(local_pairs, 'seq', axis=1, tiled=True)  143 us
    all_gather x1, waiting for transfers between devices, per_device(): lax.all_gather(embedding, 'seq', axis=0, tiled=True)  112 us
    reduce_scatter x1, waiting for transfers between devices, per_device(): lax.psum_scatter(up_weight_grad.astype(jnp.bfloat16), 'seq', scatter_dime...  98.9 us
    reduce_scatter x1, waiting for transfers between devices, per_device(): lax.psum_scatter(down_weight_grad.astype(jnp.bfloat16), 'seq', scatter_di...  98.9 us
    reduce_scatter x1, waiting for transfers between devices, per_device(): lax.psum_scatter(joint_weight_grad.astype(jnp.bfloat16), 'seq', scatter_d...  82.7 us
    all_gather x1, waiting for transfers between devices, per_device(): lax.all_gather(down_weight, 'seq', axis=0, tiled=True)  71.7 us
  transfers between devices with their start and end apart: 13, of which 12 were waited for; matrix products, arithmetic and copies ran while one was open for 9% of the time, Pallas kernels for 0%

commit v1 on v0

--- a/solution.py
+++ b/solution.py
@@ -8,6 +8,18 @@
 HEAD_DIM = 64
 EPS = 1e-05
 NEG = -1e30
+
+
+def gather_by_bits(x, axis, dim):
+    ways, here, turn = (lax.axis_size(axis), lax.axis_index(axis), x.shape[dim])
+    line, have = (x, 1)
+    while have < ways:
+        line = jnp.concatenate(
+            [line, lax.ppermute(line, axis, [(d, (d - have) % ways) for d in range(ways)])],
+            axis=dim,
+        )
+        have = 2 * have
+    return jnp.roll(line, here * turn, axis=dim)
 
 
 def layer_norm(values, gain, shift):
@@ -51,7 +63,7 @@
         lax.all_gather(embedding, "seq", axis=0, tiled=True),
         lax.all_gather(first_gain, "seq", axis=0, tiled=True),
         lax.all_gather(first_shift, "seq", axis=0, tiled=True),
-        lax.all_gather(joint_weight, "seq", axis=0, tiled=True),
+        gather_by_bits(joint_weight, "seq", 0),
         lax.all_gather(output_weight, "seq", axis=0, tiled=True),
         lax.all_gather(second_gain, "seq", axis=0, tiled=True),
         lax.all_gather(second_shift, "seq", axis=0, tiled=True),

time: 1790 us -> 1910 us (1.067)
  blocking collectives: 94.2 us -> 171 us
  waiting for transfers between devices: 1310 us -> 1330 us
    ppermute x0 -> x3, waiting for transfers between devices: none -> 123 us  [gather_by_bits(): lax.ppermute(line, axis, [(d, (d - have) % ways) for d in range(ways)])]
    all_gather x1, waiting for transfers between devices: 112 us -> 0.01 us  [per_device(): lax.all_gather(embedding, 'seq', axis=0, tiled=True)]
    unnamed x2, blocking collectives: 59.8 us -> 124 us
  transfers between devices with their start and end apart: 13 -> 16, of which waited for: 12 -> 14; matrix products, arithmetic and copies ran while one was open for 9% -> 9% of each run, Pallas kernels for 0% -> 0%
where the time goes in v1:
time: 1910 us; the launch traced here: 1900 us
  waiting for transfers between devices  1330 us (70%)
  matrix products  185 us (10%)
  blocking collectives  171 us (9%)
  local copies, waits for them, and re-layouts  88.1 us (5%)
  other arithmetic  49.9 us (3%)
  loops' own time  44.7 us (2%)
    reduce_scatter x1, waiting for transfers between devices, per_device(): lax.psum_scatter(every_pair.astype(jnp.bfloat16), 'seq', scatter_dimensio...  414 us
    reduce_scatter x1, waiting for transfers between devices, per_device(): lax.psum_scatter(embedding_grad.astype(jnp.bfloat16), 'seq', scatter_dime...  165 us
    all_gather x1, waiting for transfers between devices, per_device(): sequence_pairs = lax.all_gather(local_pairs, 'seq', axis=1, tiled=True)  146 us
    unnamed x2, blocking collectives  124 us
    ppermute x3, waiting for transfers between devices, gather_by_bits(): lax.ppermute(line, axis, [(d, (d - have) % ways) for d in range(ways)])  123 us
    reduce_scatter x1, waiting for transfers between devices, per_device(): lax.psum_scatter(up_weight_grad.astype(jnp.bfloat16), 'seq', scatter_dime...  98.9 us
    reduce_scatter x1, waiting for transfers between devices, per_device(): lax.psum_scatter(down_weight_grad.astype(jnp.bfloat16), 'seq', scatter_di...  98.8 us
    reduce_scatter x1, waiting for transfers between devices, per_device(): lax.psum_scatter(joint_weight_grad.astype(jnp.bfloat16), 'seq', scatter_d...  82.7 us
  transfers between devices with their start and end apart: 16, of which 14 were waited for; matrix products, arithmetic and copies ran while one was open for 9% of the time, Pallas kernels for 0%

profile of v1, /device:TPU:0, one launch (start us, length us, event | category | flops | bytes accessed | tf_op | source)
XLA Modules:
  0.0 1896.5 jit_solution(11239641198370974155)
XLA Ops:
  8.0 6.1 collective-permute-start
  14.1 12.2 collective-permute-done
  27.5 53.9 %collective-permute-done.1 = bf16[192,2304]{1,0:T(8,128)(2,1)S(1)} collective-permute-done((bf16[192,2304]{1,0:T(8,128)(2,1)S(1)}, bf16[192,2304]{1,0:T(8,128)(2,1)S(1)}, u32[]{:S(2)}, u32[]{:S(2)}) %collective-permute-start.1) | collective-permute-done | bytes 884768 | tf_op jit(solution)/shard_map/ppermute | solution.py:18
  86.5 88.8 %all-reduce.12 = (bf16[768]{0:T(1024)(128)(2,1)}, bf16[768]{0:T(1024)(128)(2,1)}, bf16[768]{0:T(1024)(128)(2,1)}, bf16[768]{0:T(1024)(128)(2,1)}) all-reduce(bf16[768]{0:T(1024)(128)(2,1)S(1)} %dynamic-update-slice.1, bf16[768]{0:T(1024)(128)(2,1)S(1)} %dynamic-update-slice, ...), channel_id=1, replica_groups=mesh['dp'=4,'seq'=8] {'seq'}, use_global_device_ids=true, to_apply=%add.1 | all-reduce | flops 3072 | bytes 12288
  179.3 57.2 %collective-permute-done.2 = bf16[384,2304]{1,0:T(8,128)(2,1)S(1)} collective-permute-done((bf16[384,2304]{1,0:T(8,128)(2,1)}, bf16[384,2304]{1,0:T(8,128)(2,1)S(1)}, u32[]{:S(2)}, u32[]{:S(2)}) %collective-permute-start.2) | collective-permute-done | bytes 1769504 | tf_op jit(solution)/shard_map/ppermute | solution.py:18
  241.8 9.7 fusion.83
  252.6 4.2 convolution_convert_fusion.5
  261.6 40.5 %all-gather.1 = bf16[8,1,384]{2,1,0:T(2,128)(2,1)S(1)} all-gather(bf16[1,1,384]{2,1,0:T(2,128)(2,1)S(1)} %reshape.385), channel_id=1, replica_groups=mesh['dp'=4,'seq'=8] {'seq'}, dimensions={0}, use_global_device_ids=true | all-gather | bytes 6912 | tf_op jit(solution)/shard_map/all_gather | solution.py:71
  305.1 145.7 %all-gather.19.cloned.1.call-done = bf16[4096,1536]{1,0:T(8,128)(2,1)} async-done(((bf16[512,1536]{1,0:T(8,128)(2,1)}), bf16[4096,1536]{1,0:T(8,128)(2,1)}) %all-gather.19.cloned.1.call-update) | async-done | bytes 12582928 | tf_op jit(solution)/shard_map/all_gather | solution.py:96
  450.8 10.3 fusion.81
  461.1 8.8 copy.68
  469.9 8.6 copy.67
  478.5 35.6 %while.38 = (s32[]{:T(128)}, f32[1,12,512]{2,1,0:T(8,128)S(1)}, f32[1,12,512]{2,1,0:T(8,128)S(1)}, s32[8]{0:T(128)S(1)}, s32[]{:T(128)}, /*index=5*/s32[1,4096]{...) while((s32[]{:T(128)}, f32[1,12,512]{2,1,0:T(8,128)S(1)}, ...), condition=%wide.region_8.9_spmd, body=%wide.region_3.8_spmd.sunk | while | flops 424947712 | bytes 27853072 | solution.py:128
  480.4 10.1 conditional.7
  482.7 5.2 fusion
  488.0 2.6 exponential_reduce_fusion
  492.5 10.1 conditional.7
  494.7 5.2 fusion
  514.4 33.7 %while.39 = (s32[]{:T(128)}, f32[1,512,12,64]{1,3,2,0:T(8,128)S(1)}, s32[8]{0:T(128)S(1)}, s32[]{:T(128)}, bf16[1,4096,12,64]{1,3,2,0:T(8,128)(2,1)}, /*index=5*...) while((s32[]{:T(128)}, ...), condition=%wide.region_12.13_spmd, body=%wide.region_9.12_spmd.sunk | while | flops 818544640 | bytes 6063357 | solution.py:145
  516.3 8.9 conditional.8
  518.5 6.7 bitcast_add_fusion.1
  527.1 9.0 conditional.8
  529.4 6.7 bitcast_add_fusion.1
  552.9 19.5 %all-gather.13.cloned.1.call-done = bf16[768,3072]{1,0:T(8,128)(2,1)} async-done(((bf16[96,3072]{1,0:T(8,128)(2,1)}), bf16[768,3072]{1,0:T(8,128)(2,1)}) %all-gather.13.cloned.1.call-update) | async-done | bytes 4718608 | tf_op jit(solution)/shard_map/all_gather | solution.py:70
  572.4 8.1 fusion.78
  580.5 71.7 %all-gather.15.cloned.1.call-done = bf16[3072,768]{1,0:T(8,128)(2,1)} async-done(((bf16[384,768]{1,0:T(8,128)(2,1)}), bf16[3072,768]{1,0:T(8,128)(2,1)}) %all-gather.15.cloned.1.call-update) | async-done | bytes 4718608 | tf_op jit(solution)/shard_map/all_gather | solution.py:72
  652.2 9.8 fusion.85
  662.0 3.5 multiply_reduce_fusion
  671.9 125.4 %while.40 = (s32[]{:T(128)}, f32[1,512,12,64]{1,3,2,0:T(8,128)}, bf16[8,512,1,1536]{3,1,0,2:T(8,128)(2,1)}, s32[8]{0:T(128)S(1)}, s32[]{:T(128)}, /*index=5*/bf1...) while((s32[]{:T(128)}, f32[1,512,12,64]{1,3,2,0:T(8,128)}, ...), condition=%wide.region_21.22_spmd.clone, body=%wide.region_18.21_spmd.clone.sunk | while | flops 2050097152 | bytes 80298304 | solution.py:253
  673.9 35.1 %conditional.9 = (f32[1,512,12,64]{1,3,2,0:T(8,128)S(1)}, bf16[1,512,1,1536]{1,3,2,0:T(8,128)(2,1)S(1)}) conditional(s32[]{:T(128)} %convert_element_type.293, () %tuple.107, (s32[]{:T(128)}, bf16[1,4096,12,64]{1,3,2,0:T(8,128)(2,1)}, s32[1,4096]{1,0:T(1,128)S(1)}, s32[1,512]{1,0:T(1,128)S(1)}, bf16[1,512,12,64]{1,3,2,0:T(8,128)(2,1)}, ...), branch_computations={%region_19.19_spmd, %region_20.20_spmd} | conditional | flops 2049310720 | bytes 69288000 | solution.py:248
  676.2 9.5 fusion.39
  685.7 9.7 fusion.28
  695.5 7.8 fusion.32
  705.8 3.1 convolution_multiply_fusion
  714.4 35.1 %conditional.9 = (f32[1,512,12,64]{1,3,2,0:T(8,128)S(1)}, bf16[1,512,1,1536]{1,3,2,0:T(8,128)(2,1)S(1)}) conditional(s32[]{:T(128)} %convert_element_type.293, () %tuple.107, (s32[]{:T(128)}, bf16[1,4096,12,64]{1,3,2,0:T(8,128)(2,1)}, s32[1,4096]{1,0:T(1,128)S(1)}, s32[1,512]{1,0:T(1,128)S(1)}, bf16[1,512,12,64]{1,3,2,0:T(8,128)(2,1)}, ...), branch_computations={%region_19.19_spmd, %region_20.20_spmd} | conditional | flops 2049310720 | bytes 69288000 | solution.py:248
  716.7 9.6 fusion.39
  726.2 9.7 fusion.28
  735.9 7.8 fusion.32
  746.2 3.1 convolution_multiply_fusion
  749.5 2.9 select_add_fusion.2
  756.6 2.9 select_add_fusion.2
  763.6 2.9 select_add_fusion.2
  770.8 2.9 select_add_fusion.2
  777.9 2.9 select_add_fusion.2
  785.0 2.9 select_add_fusion.2
  792.1 2.9 select_add_fusion.2
  800.5 6.5 convolution_convert_fusion.3
  808.1 8.6 convolution_convert_fusion.2
  820.4 414.2 %reduce-scatter.7.cloned.1.call-done = bf16[512,1,1536]{2,0,1:T(8,128)(2,1)} async-done(((bf16[4096,1,1536]{2,0,1:T(8,128)(2,1)}), bf16[512,1,1536]{2,0,1:T(8,128)(2,1)}) %reduce-scatter.7.cloned.1.call-update) | async-done | bytes 1572880 | tf_op jit(solution)/shard_map/reduce_scatter | solution.py:255
  1234.6 5.4 convolution_convert_fusion.4
  1240.1 60.4 %all-gather.17.cloned.1.call-done = bf16[768,2304]{1,0:T(8,128)(2,1)} async-done(((bf16[96,2304]{1,0:T(8,128)(2,1)}), bf16[768,2304]{1,0:T(8,128)(2,1)}) %all-gather.17.cloned.1.call-update) | async-done | bytes 3538960 | tf_op jit(solution)/shard_map/all_gather | solution.py:163
  1300.5 4.8 multiply_reduce_fusion.1
  1307.3 10.6 fusion.51
  1319.8 34.9 %all-reduce.11 = (bf16[768]{0:T(1024)(128)(2,1)S(1)}, bf16[768]{0:T(1024)(128)(2,1)S(1)}, bf16[768]{0:T(1024)(128)(2,1)S(1)}, bf16[768]{0:T(1024)(128)(2,1)S(1)}...) all-reduce(bf16[768]{0:T(1024)(128)(2,1)S(1)} %dynamic-update-slice, ...), channel_id=1, replica_groups=mesh['dp'=4,'seq'=8] {'seq'}, use_global_device_ids=true, to_apply=%add.4 | all-reduce | flops 7680 | bytes 30720
  1354.7 13.3 reduce-scatter.13.cloned.1.call-done
  1368.0 98.9 %reduce-scatter.15.cloned.1.call-done = bf16[96,3072]{1,0:T(8,128)(2,1)} async-done(((bf16[768,3072]{1,0:T(8,128)(2,1)}), bf16[96,3072]{1,0:T(8,128)(2,1)}) %reduce-scatter.15.cloned.1.call-update) | async-done | bytes 589840 | tf_op jit(solution)/shard_map/reduce_scatter | solution.py:296
  1466.9 98.8 %reduce-scatter.17.cloned.1.call-done = bf16[384,768]{1,0:T(8,128)(2,1)} async-done(((bf16[3072,768]{1,0:T(8,128)(2,1)}), bf16[384,768]{1,0:T(8,128)(2,1)}) %reduce-scatter.17.cloned.1.call-update) | async-done | bytes 589840 | tf_op jit(solution)/shard_map/reduce_scatter | solution.py:302
  1565.7 82.7 %reduce-scatter.11.cloned.1.call-done = bf16[96,2304]{1,0:T(8,128)(2,1)} async-done(((bf16[768,2304]{1,0:T(8,128)(2,1)}), bf16[96,2304]{1,0:T(8,128)(2,1)}) %reduce-scatter.11.cloned.1.call-update) | async-done | bytes 442384 | tf_op jit(solution)/shard_map/reduce_scatter | solution.py:284
  1648.4 165.2 %reduce-scatter.9.cloned.1.call-done = bf16[768,768]{0,1:T(8,128)(2,1)} async-done(((bf16[6144,768]{0,1:T(8,128)(2,1)}), bf16[768,768]{0,1:T(8,128)(2,1)}) %reduce-scatter.9.cloned.1.call-update) | async-done | bytes 1179664 | tf_op jit(solution)/shard_map/reduce_scatter | solution.py:275
  1813.6 9.0 fusion.65
  1823.1 7.3 all-reduce.13
  1833.5 10.8 fusion.52
  1844.3 36.6 %all-reduce.17.cloned.1.call-done = (bf16[768,768]{0,1:T(8,128)(2,1)}, bf16[96,2304]{1,0:T(8,128)(2,1)}, bf16[96,768]{1,0:T(8,128)(2,1)}, bf16[96,3072]{1,0:T(8,128)(2,1)}, bf16[384,768]{1,0:T(8,128)(2,1)}) async-done(((bf16[768,768]{0,1:T(8,128)(2,1)}, bf16[96,2304]{1,0:T(8,128)(2,1)}, bf16[96,768]{1,0:T(8,128)(2,1)}, bf16[96,3072]{1,0:T(8,128)(2,1)}, bf16[384,768]{1,0:T(8,128)(2,1)}), ...) | async-done | bytes 2949136 | tf_op jit(solution)/shard_map/psum | solution.py:310
  1884.6 2.7 copy.73
  (307 shorter events, 100.4 us)
Async XLA Ops:
  7.2 76.5 %copy-start.43 = (u32[32]{0:T(128)S(1)}, u32[32]{0:T(128)}, u32[]{:S(2)}) copy-start(u32[32]{0:T(128)} %constant.120) | copy-start | bytes 388
  7.2 169.5 %copy-start.9 = (bf16[96,2304]{1,0:T(8,128)(2,1)S(1)}, bf16[96,2304]{1,0:T(8,128)(2,1)}, u32[]{:S(2)}) copy-start(bf16[96,2304]{1,0:T(8,128)(2,1)} %param.30) | copy-start | bytes 1327108
  7.2 77.7 %copy-start.46 = (bf16[96]{0:T(256)(128)(2,1)S(1)}, bf16[96]{0:T(256)(128)(2,1)}, u32[]{:S(2)}) copy-start(bf16[96]{0:T(256)(128)(2,1)} %param.32) | copy-start | bytes 580
  7.2 78.0 %copy-start.47 = (bf16[96]{0:T(256)(128)(2,1)S(1)}, bf16[96]{0:T(256)(128)(2,1)}, u32[]{:S(2)}) copy-start(bf16[96]{0:T(256)(128)(2,1)} %param.33) | copy-start | bytes 580
  7.2 78.2 %copy-start.48 = (bf16[96]{0:T(256)(128)(2,1)S(1)}, bf16[96]{0:T(256)(128)(2,1)}, u32[]{:S(2)}) copy-start(bf16[96]{0:T(256)(128)(2,1)} %param.28) | copy-start | bytes 580
  7.2 234.5 %all-gather.9.cloned.1.call-start = ((), (), s32[]{:S(2)}) async-start(), calls=%async_computation.6 | async-start | bytes 10616832 | tf_op jit(solution)/shard_map/all_gather | solution.py:63
  8.0 442.8 %all-gather.19.cloned.1.call-start = ((), (), s32[]{:S(2)}) async-start(), calls=%async_computation.17 | async-start | bytes 14155776 | tf_op jit(solution)/shard_map/all_gather | solution.py:96
  8.0 18.3 collective-permute-start
  27.4 53.9 %collective-permute-start.1 = (bf16[192,2304]{1,0:T(8,128)(2,1)S(1)}, bf16[192,2304]{1,0:T(8,128)(2,1)S(1)}, u32[]{:S(2)}, u32[]{:S(2)}) collective-permute-start(bf16[192,2304]{1,0:T(8,128)(2,1)S(1)} %pad_maximum_fusion.4), channel_id=1, source_target_pairs={{0,6},{1,7},{2,0},{3,1},{4,2},{5,3},{6,4},{7,5},{8,14},{9,15},{10,... | collective-permute-start | bytes 2654216 | tf_op jit(solution)/shard_map/ppermute | solution.py:18
  83.7 152.8 %collective-permute-start.2 = (bf16[384,2304]{1,0:T(8,128)(2,1)}, bf16[384,2304]{1,0:T(8,128)(2,1)S(1)}, u32[]{:S(2)}, u32[]{:S(2)}) collective-permute-start(bf16[384,2304]{1,0:T(8,128)(2,1)} %pad_maximum_fusion.1), channel_id=1, source_target_pairs={{0,4},{1,5},{2,6},{3,7},{4,0},{5,1},{6,2},{7,3},{8,12},{9,13},{10,... | collective-permute-start | bytes 5308424 | tf_op jit(solution)/shard_map/ppermute | solution.py:18
  176.0 76.6 %copy-start.35 = (f32[768]{0:T(1024)}, f32[768]{0:T(1024)S(1)}, u32[]{:S(2)}) copy-start(f32[768]{0:T(1024)S(1)} %convert_element_type.201) | copy-start | bytes 9220
  176.7 75.9 %copy-start.28 = (f32[768]{0:T(1024)}, f32[768]{0:T(1024)S(1)}, u32[]{:S(2)}) copy-start(f32[768]{0:T(1024)S(1)} %convert_element_type.200) | copy-start | bytes 9220
  251.5 297.5 %copy-start.1 = (f32[512,768]{1,0:T(8,128)}, f32[512,768]{1,0:T(8,128)S(1)}, u32[]{:S(2)}) copy-start(f32[512,768]{1,0:T(8,128)S(1)} %get-tuple-element.512) | copy-start | bytes 4718596
  251.5 5.3 copy-start.22
  252.6 4.2 copy-start.32
  256.8 1.4 copy-start.15
  258.2 3.3 copy-start.44
  258.2 3.3 copy-start.42
  258.2 3.3 copy-start.41
  258.2 43.8 %copy-start.21 = (s32[1,4096]{1,0:T(1,128)S(1)}, s32[1,4096]{1,0:T(1,128)}, u32[]{:S(2)}) copy-start(s32[1,4096]{1,0:T(1,128)} %param.38) | copy-start | bytes 49156
  259.5 44.5 %slice-start = ((bf16[512,2304]{1,0:T(8,128)(2,1)}), bf16[512,768]{1,0:T(8,128)(2,1)S(1)}, s32[]{:S(2)}) async-start(bf16[512,2304]{1,0:T(8,128)(2,1)} %copy-done.15), calls=%async_computation.19 | async-start | bytes 1572864 | tf_op jit(solution)/shard_map/slice | solution.py:94
  259.5 289.5 %all-gather.11.cloned.1.call-start = ((), (), s32[]{:S(2)}) async-start(), calls=%async_computation.7 | async-start | bytes 1327104 | tf_op jit(solution)/shard_map/all_gather | solution.py:67
  260.3 312.1 %all-gather.13.cloned.1.call-start = ((), (), s32[]{:S(2)}) async-start(), calls=%async_computation.8 | async-start | bytes 5308416 | tf_op jit(solution)/shard_map/all_gather | solution.py:70
  260.8 391.3 %all-gather.15.cloned.1.call-start = ((), (), s32[]{:S(2)}) async-start(), calls=%async_computation.9 | async-start | bytes 5308416 | tf_op jit(solution)/shard_map/all_gather | solution.py:72
  261.4 973.2 %reduce-scatter.7.cloned.1.call-start = ((), (), s32[]{:S(2)}) async-start(), calls=%async_computation.10 | async-start | bytes 14155776 | tf_op jit(solution)/shard_map/reduce_scatter | solution.py:255
  261.6 310.8 %copy-start.37 = (f32[768]{0:T(1024)}, f32[768]{0:T(1024)S(1)}, u32[]{:S(2)}) copy-start(f32[768]{0:T(1024)S(1)} %convert_element_type.207) | copy-start | bytes 9220
  302.0 350.1 %copy-start.30 = (f32[8,1,384]{2,1,0:T(1,128)}, f32[8,1,384]{2,1,0:T(1,128)S(1)}, u32[]{:S(2)}) copy-start(f32[8,1,384]{2,1,0:T(1,128)S(1)} %convert_element_type.243) | copy-start | bytes 36868
  551.5 1.1 copy-start.3
  552.9 99.3 %copy-start.10 = (bf16[1,512,768]{2,1,0:T(8,128)(2,1)S(1)}, bf16[1,512,768]{2,1,0:T(8,128)(2,1)}, u32[]{:S(2)}) copy-start(bf16[1,512,768]{2,1,0:T(8,128)(2,1)} %param.39) | copy-start | bytes 2359300
  652.2 9.8 copy-start.4
  652.2 9.8 copy-start.45
  662.0 3.5 copy-start.50
  665.5 3.0 copy-start.16
  666.2 1.1 copy-start.7
  666.2 4.3 copy-start.26
  797.2 1.1 copy-start.14
  797.2 1.4 copy-start.18
  797.3 3.2 copy-start.5
  797.3 3.2 copy-start.38
  797.3 503.2 %all-gather.17.cloned.1.call-start = ((), (), s32[]{:S(2)}) async-start(), calls=%async_computation.11 | async-start | bytes 3981312 | tf_op jit(solution)/shard_map/all_gather | solution.py:163
  798.0 570.0 %reduce-scatter.13.cloned.1.call-start = ((), (), s32[]{:S(2)}) async-start(), calls=%async_computation.14 | async-start | bytes 1327104 | tf_op jit(solution)/shard_map/reduce_scatter | solution.py:287
  800.4 666.5 %reduce-scatter.15.cloned.1.call-start = ((), (), s32[]{:S(2)}) async-start(), calls=%async_computation.15 | async-start | bytes 5308416 | tf_op jit(solution)/shard_map/reduce_scatter | solution.py:296
  807.0 758.7 %reduce-scatter.17.cloned.1.call-start = ((), (), s32[]{:S(2)}) async-start(), calls=%async_computation.16 | async-start | bytes 5308416 | tf_op jit(solution)/shard_map/reduce_scatter | solution.py:302
  816.6 1.4 copy-start
  816.6 418.0 %copy-start.2 = (f32[512,768]{1,0:T(8,128)S(1)}, f32[512,768]{1,0:T(8,128)}, u32[]{:S(2)}) copy-start(f32[512,768]{1,0:T(8,128)} %copy-done.1) | copy-start | bytes 4718596
  816.6 418.0 %copy-start.23 = (f32[512]{0:T(512)S(1)}, f32[512]{0:T(512)}, u32[]{:S(2)}) copy-start(f32[512]{0:T(512)} %copy-done.22) | copy-start | bytes 6148
  816.6 418.0 %copy-start.29 = (f32[768]{0:T(1024)S(1)}, f32[768]{0:T(1024)}, u32[]{:S(2)}) copy-start(f32[768]{0:T(1024)} %copy-done.28) | copy-start | bytes 9220
  816.6 418.0 %copy-start.33 = (f32[512]{0:T(512)S(1)}, f32[512]{0:T(512)}, u32[]{:S(2)}) copy-start(f32[512]{0:T(512)} %copy-done.32) | copy-start | bytes 6148
  816.6 418.0 %copy-start.36 = (f32[768]{0:T(1024)S(1)}, f32[768]{0:T(1024)}, u32[]{:S(2)}) copy-start(f32[768]{0:T(1024)} %copy-done.35) | copy-start | bytes 9220
  816.7 831.7 %reduce-scatter.11.cloned.1.call-start = ((), (), s32[]{:S(2)}) async-start(), calls=%async_computation.13 | async-start | bytes 3981312 | tf_op jit(solution)/shard_map/reduce_scatter | solution.py:284
  1240.1 65.2 %copy-start.25 = (f32[512]{0:T(512)S(1)}, f32[512]{0:T(512)}, u32[]{:S(2)}) copy-start(f32[512]{0:T(512)} %copy-done.24) | copy-start | bytes 6148
  1240.1 573.5 %reduce-scatter.9.cloned.1.call-start = ((), (), s32[]{:S(2)}) async-start(), calls=%async_computation.12 | async-start | bytes 10616832 | tf_op jit(solution)/shard_map/reduce_scatter | solution.py:275
  1305.3 1.4 copy-start.8
  1305.3 1.6 copy-start.12
  1305.3 1.6 copy-start.27
  1317.8 1.6 copy-start.13
  1317.8 1.7 copy-start.49
  1317.8 2.0 copy-start.34
  1317.8 2.0 copy-start.39
  1317.8 2.0 copy-start.40
  1317.9 495.8 %copy-start.6 = (f32[512,768]{1,0:T(8,128)S(1)}, f32[512,768]{1,0:T(8,128)}, u32[]{:S(2)}) copy-start(f32[512,768]{1,0:T(8,128)} %copy-done.3) | copy-start | bytes 4718596
  1317.9 563.0 %all-reduce.17.cloned.1.call-start = ((), (), s32[]{:S(2)}) async-start(), calls=%async_computation.18 | async-start | bytes 5898240 | tf_op jit(solution)/shard_map/psum | solution.py:310
  1880.9 6.4 copy-start.20
  1880.9 7.5 copy-start.19
  (4 other events, 3.9 us)
Sparse Core Ops, SparseCore 0:
  10.2 226.7 all-gather.8
  259.7 191.1 all-gather.18
  453.0 39.2 all-gather.10
  494.4 77.9 all-gather.12
  574.4 77.6 all-gather.14
  797.4 437.1 reduce-scatter.6
  1236.8 63.6 all-gather.16
  1304.5 63.5 reduce-scatter.12
  1372.3 94.5 reduce-scatter.14
  1470.4 95.2 reduce-scatter.16
  1569.3 79.0 reduce-scatter.10
  1651.8 161.7 reduce-scatter.8
  1816.3 64.5 all-reduce.16
